TPU v7x, 32 devices: a whole 2x2x4 slice. The times are simulated.
32 devices in a mesh: visit: 8 (over y, x, core), sky: 4 (over z).
Axes of the slice: x: 2, y: 2, z: 4, core: 2. Of those that a mesh axis runs over, the one named last changes fastest.
Arguments:
- science: float32 [8, 16, 128, 128], P('visit', 'sky'), may hold values from -6 to 6
- coef_first: float32 [8, 16, 3, 49], P('visit', 'sky'), may hold values from -4 to 4
- coef_second: float32 [8, 16, 3, 49], P('visit', 'sky'), may hold values from -4 to 4
- weight: float32 [8, 16], P('visit', 'sky'), may hold values from 0.3 to 3
- slot_tile: int32 [8, 16], P('visit', 'sky'), may hold values from 0 to 3, as said below
- offsets: int32 [8, 16, 2], P('visit', 'sky'), may hold values from 0 to 128
- counts: int32 [8, 4], P('visit', 'sky'), may hold values from 3 to 4, as said below
- tile_place: int32 [4], replicated, may hold values from 0 to 3, as said below
Outputs:
- template: float32 [4, 256, 256], P('sky')
- difference: float32 [8, 16, 128, 128], P('visit', 'sky')
Inputs may be any that keep to these rules, and one draw needn't show every extreme that they name: `slot_tile`: among the usable slots of one device's list at most 2 name tiles of one owner; in every visit the tile of some owner gets exactly 2 usable slots from every device of the sky axis. A permutation: tile t is owned by the device of sky index tile_place[t]. The first counts[v, s] slots of a device's list are usable; in every visit some device has all 4 usable.
All inputs are finite; a program needn't handle non-finite values.
Results may differ from a plain program's by a relative error of at most 0.00011.
Values sent between devices are 32-bit elements; how exact they have to be, the bound alone decides.
No kernel may reach another device: no remote copies, remote signals or barrier semaphores. Data moves between devices by JAX's collectives and lax.ppermute only.
A program may use at most 64 MiB of HBM per device.

v0:
```python
import jax
import jax.numpy as jnp
from jax import lax
from jax.sharding import PartitionSpec as P

TILE = 256
TAPS = 21
PROFILES = 7
WIDTHS = (1.0, 1.0, 1.0, 2.5, 2.5, 2.5, 5.0)
POWERS = (0, 1, 2, 0, 1, 2, 0)
PRECISE = lax.Precision.HIGHEST


def profile_filters(side):
    reach = (TAPS - 1) // 2
    places = jnp.arange(side).astype(jnp.float32)
    spacing = places[None, :] - places[:, None]
    support = jnp.arange(TAPS).astype(jnp.float32) - reach
    stacked = []
    for number in range(PROFILES):
        sample = support ** POWERS[number] * jnp.exp(
            -support * support / (2.0 * WIDTHS[number] ** 2)
        )
        norming = jnp.sqrt(jnp.sum(sample * sample))
        values = spacing ** POWERS[number] * jnp.exp(
            -spacing * spacing / (2.0 * WIDTHS[number] ** 2)
        )
        stacked.append(jnp.where(jnp.abs(spacing) <= reach, values / norming, 0.0))
    return jnp.stack(stacked)


def positions(side):
    places = jnp.arange(side).astype(jnp.float32)
    return (2.0 * places - (side - 1)) / (side - 1)


def kernel_pass(block, coeffs, filters, spread):
    across_x = jnp.einsum("yw,ixw->iyx", block, filters, precision=PRECISE)
    layout = coeffs.reshape(3, PROFILES, PROFILES)
    plain = jnp.einsum("ij,jab->iab", layout[0], filters, precision=PRECISE)
    along = jnp.einsum("ij,jab->iab", layout[2], filters, precision=PRECISE) * spread[None, :, None]
    sideways = jnp.einsum("ij,jab->iab", layout[1], filters, precision=PRECISE)
    steady = jnp.einsum("iab,ibx->ax", plain + along, across_x, precision=PRECISE)
    varying = jnp.einsum("iab,ibx->ax", sideways, across_x, precision=PRECISE)
    return steady + varying * spread[None, :]


def body(science, coef_first, coef_second, weight, slot_tile, offsets, counts, tile_place):
    slots = science.shape[1]
    side = science.shape[2]
    owners_count = lax.axis_size("sky")
    capacity = max(2, (slots + owners_count - 1) // owners_count)
    buffer_slots = owners_count * capacity
    filters = profile_filters(side)
    spread = positions(side)
    listed = jnp.arange(slots)
    usable = listed < counts[0, 0]
    tile_ids = jnp.arange(tile_place.shape[0])
    owners = jnp.sum(
        jnp.where(slot_tile[0][:, None] == tile_ids[None, :], tile_place[None, :], 0), axis=1
    )
    convolved = lax.map(
        lambda operands: kernel_pass(operands[0], operands[1], filters, spread),
        (science[0], coef_first[0]),
    )
    sharing = (
        (owners[:, None] == owners[None, :]) & usable[None, :] & (listed[None, :] < listed[:, None])
    )
    earlier = jnp.sum(sharing.astype(jnp.int32), axis=1)
    target = jnp.where(usable, owners * capacity + earlier, -1)
    routing = (target[None, :] == jnp.arange(buffer_slots)[:, None]).astype(jnp.float32)
    packed = jnp.dot(routing, convolved.reshape(slots, side * side), precision=PRECISE).reshape(
        buffer_slots, side, side
    )
    sent_weight = jnp.dot(routing, weight[0], precision=PRECISE)
    sent_corner = jnp.dot(routing, offsets[0].astype(jnp.float32), precision=PRECISE)
    arrived, arrived_weight, arrived_corner = (
        lax.all_to_all(packed, "sky", split_axis=0, concat_axis=0, tiled=True),
        lax.all_to_all(sent_weight, "sky", split_axis=0, concat_axis=0, tiled=True),
        lax.all_to_all(sent_corner, "sky", split_axis=0, concat_axis=0, tiled=True),
    )
    corners = arrived_corner.astype(jnp.int32)

    def place_block(position, totals):
        weighted, coverage = totals
        corner_top = corners[position, 0]
        corner_left = corners[position, 1]
        block_weight = arrived_weight[position]
        region = lax.dynamic_slice(weighted, (corner_top, corner_left), (side, side))
        weighted = lax.dynamic_update_slice(
            weighted, region + block_weight * arrived[position], (corner_top, corner_left)
        )
        region = lax.dynamic_slice(coverage, (corner_top, corner_left), (side, side))
        coverage = lax.dynamic_update_slice(
            coverage, region + block_weight, (corner_top, corner_left)
        )
        return (weighted, coverage)

    empty = jnp.zeros((TILE, TILE), jnp.float32)
    weighted, coverage = lax.fori_loop(0, buffer_slots, place_block, (empty, empty))
    weighted, coverage = lax.psum((weighted, coverage), "visit")
    template = weighted / (coverage + 1.0)
    cut_back = jax.vmap(
        lambda corner: lax.dynamic_slice(template, (corner[0], corner[1]), (side, side))
    )(corners)
    returned = lax.all_to_all(cut_back, "sky", split_axis=0, concat_axis=0, tiled=True)
    cutouts = jnp.dot(
        routing.T, returned.reshape(buffer_slots, side * side), precision=PRECISE
    ).reshape(slots, side, side)
    matched = lax.map(
        lambda operands: kernel_pass(operands[0], operands[1], filters, spread),
        (cutouts, coef_second[0]),
    )
    difference = jnp.where(usable[:, None, None], science[0] - matched, 0.0)
    return (template[None], difference[None])


def solution(mesh):
    in_specs = (
        P("visit", "sky", None, None),
        P("visit", "sky", None, None),
        P("visit", "sky", None, None),
        P("visit", "sky"),
        P("visit", "sky"),
        P("visit", "sky", None),
        P("visit", "sky"),
        P(),
    )
    out_specs = (P("sky", None, None), P("visit", "sky", None, None))
    return jax.shard_map(body, mesh=mesh, in_specs=in_specs, out_specs=out_specs, check_vma=False)
```

profile of v0, /device:TPU:0, one launch (start us, length us, event | category | flops | bytes accessed | tf_op | source)
XLA Modules:
  0.0 270.1 jit_solution(13443177923790171623)
XLA Ops:
  9.8 6.3 %all-to-all-start.1 = ((f32[4,2,1]{1,2,0:T(1,128)}), f32[4,2,1]{1,2,0:T(1,128)S(1)}, u32[]{:S(2)}, u32[]{:S(2)}) async-start(f32[4,2,1]{1,2,0:T(1,128)} %copy.57), calls=%async_computation.1 | async-start | bytes 4096 | tf_op jit(solution)/shard_map/all_to_all | solution.py:79
  26.9 0.9 copy-done.4
  27.8 15.7 %while.42 = (s32[]{:T(128)}, f32[4,128,128]{2,1,0:T(8,128)S(1)}, f32[4,3,49]{2,1,0:T(4,128)S(1)}, f32[7,128,128]{2,0,1:T(8,128)S(1)}, f32[4,128,128]{2,1,0:T(8,128)S(1)}, /*index=5*/s32[]{:T(128)}) while((s32[]{:T(128)}, f32[4,128,128]{2,1,0:T(8,128)S(1)}, f32[4,3,49]{2,1,0:T(4,128)S(1)}, ...), condition=%wide.region_10.11_spmd.clone.clone, body=%wide.region_9.10_spmd.clone.clone.sunk | while | flops 557646336 | bytes 6362725 | solution.py:62
  45.0 5.1 %all-to-all-start = ((f32[4,2,2]{2,1,0:T(2,128)}), f32[4,2,2]{2,1,0:T(2,128)S(1)}, u32[]{:S(2)}, u32[]{:S(2)}) async-start(f32[4,2,2]{2,1,0:T(2,128)} %fusion.28), calls=%async_computation | async-start | bytes 8192 | tf_op jit(solution)/shard_map/all_to_all | solution.py:80
  50.1 0.9 copy.59
  51.0 4.7 %all-to-all-done = f32[4,2,2]{2,1,0:T(2,128)S(1)} async-done(((f32[4,2,2]{2,1,0:T(2,128)}), f32[4,2,2]{2,1,0:T(2,128)S(1)}, u32[]{:S(2)}, u32[]{:S(2)}) %all-to-all-start) | async-done | bytes 96 | tf_op jit(solution)/shard_map/all_to_all | solution.py:80
  55.6 3.5 %all-to-all-start.2 = ((f32[8,128,128]{2,1,0:T(8,128)}), f32[8,128,128]{2,1,0:T(8,128)S(1)}, u32[]{:S(2)}, u32[]{:S(2)}) async-start(f32[8,128,128]{2,1,0:T(8,128)} %copy.59), calls=%async_computation.2 | async-start | bytes 1048576 | tf_op jit(solution)/shard_map/all_to_all | solution.py:78
  60.7 11.1 %all-to-all-done.2 = f32[8,128,128]{2,1,0:T(8,128)S(1)} async-done(((f32[8,128,128]{2,1,0:T(8,128)}), f32[8,128,128]{2,1,0:T(8,128)S(1)}, u32[]{:S(2)}, u32[]{:S(2)}) %all-to-all-start.2) | async-done | bytes 524320 | tf_op jit(solution)/shard_map/all_to_all | solution.py:78
  71.9 77.3 %while.40 = (s32[]{:T(128)}, f32[256,256]{1,0:T(8,128)S(1)}, f32[256,256]{1,0:T(8,128)S(1)}, s32[8,2]{0,1:T(2,128)S(1)}, f32[8]{0:T(128)S(1)}, /*index=5*/f32[8,...) while((s32[]{:T(128)}, f32[256,256]{1,0:T(8,128)S(1)}, f32[256,256]{1,0:T(8,128)S(1)}, ...), condition=%wide.region_12.13_spmd, body=%wide.region_11.12_spmd.sunk | while | flops 49160 | bytes 591569 | solution.py:100
  77.2 0.8 bitcast_add_fusion.2
  78.0 2.0 dynamic_update_slice.32
  79.9 2.0 dynamic_update_slice.31
  87.2 0.8 bitcast_add_fusion.2
  88.0 1.9 dynamic_update_slice.32
  89.9 1.9 dynamic_update_slice.31
  97.2 0.8 bitcast_add_fusion.2
  97.9 2.0 dynamic_update_slice.32
  99.9 2.0 dynamic_update_slice.31
  107.2 0.8 bitcast_add_fusion.2
  107.9 1.7 dynamic_update_slice.32
  109.6 1.7 dynamic_update_slice.31
  116.6 0.8 bitcast_add_fusion.2
  117.3 1.9 dynamic_update_slice.32
  119.2 1.9 dynamic_update_slice.31
  126.4 0.8 bitcast_add_fusion.2
  127.1 1.7 dynamic_update_slice.32
  128.8 1.7 dynamic_update_slice.31
  135.8 0.8 bitcast_add_fusion.2
  136.5 1.7 dynamic_update_slice.32
  138.2 1.7 dynamic_update_slice.31
  145.1 0.8 bitcast_add_fusion.2
  145.9 1.7 dynamic_update_slice.32
  147.6 1.7 dynamic_update_slice.31
  150.1 54.8 %all-reduce.3.cloned.1.call-done = (f32[256,256]{1,0:T(8,128)}, f32[256,256]{1,0:T(8,128)}) async-done(((f32[256,256]{1,0:T(8,128)}, f32[256,256]{1,0:T(8,128)}), (f32[256,256]{1,0:T(8,128)}, f32[256,256]{1,0:T(8,128)})) %all-reduce.3.cloned.1.call-update) | async-done | bytes 524304 | tf_op jit(solution)/shard_map/psum | solution.py:101
  204.9 1.1 add_divide_fusion
  205.9 20.8 %while.41 = (s32[]{:T(128)}, f32[256,256]{1,0:T(8,128)S(1)}, s32[8,2]{0,1:T(2,128)S(1)}, f32[8,128,128]{2,1,0:T(8,128)}, s32[]{:T(128)}) while((s32[]{:T(128)}, f32[256,256]{1,0:T(8,128)S(1)}, s32[8,2]{0,1:T(2,128)S(1)}, f32[8,128,128]{2,1,0:T(8,128)}, s32[]{:T(128)}) %tuple.118), condition=%wide.while_cond, body=%wide.while_body.sunk | while | flops 2 | bytes 132705 | solution.py:104
  206.6 2.0 bitcast_dynamic-update-slice_fusion.2
  209.2 2.0 bitcast_dynamic-update-slice_fusion.2
  211.8 2.0 bitcast_dynamic-update-slice_fusion.2
  214.4 2.0 bitcast_dynamic-update-slice_fusion.2
  217.0 2.0 bitcast_dynamic-update-slice_fusion.2
  219.5 2.0 bitcast_dynamic-update-slice_fusion.2
  222.2 2.0 bitcast_dynamic-update-slice_fusion.2
  224.8 2.0 bitcast_dynamic-update-slice_fusion.2
  227.5 4.6 %all-to-all-start.3 = ((f32[8,128,128]{2,1,0:T(8,128)}), f32[8,128,128]{2,1,0:T(8,128)S(1)}, u32[]{:S(2)}, u32[]{:S(2)}) async-start(f32[8,128,128]{2,1,0:T(8,128)} %get-tuple-element.193), calls=%async_computation.3 | async-start | bytes 1048576 | tf_op jit(solution)/shard_map/all_to_all | solution.py:106
  232.0 13.8 %all-to-all-done.3 = f32[8,128,128]{2,1,0:T(8,128)S(1)} async-done(((f32[8,128,128]{2,1,0:T(8,128)}), f32[8,128,128]{2,1,0:T(8,128)S(1)}, u32[]{:S(2)}, u32[]{:S(2)}) %all-to-all-start.3) | async-done | bytes 524320 | tf_op jit(solution)/shard_map/all_to_all | solution.py:106
  246.5 16.0 %while.43 = (s32[]{:T(128)}, f32[4,128,128]{2,1,0:T(8,128)S(1)}, f32[4,3,49]{2,1,0:T(4,128)S(1)}, f32[7,128,128]{2,0,1:T(8,128)S(1)}, f32[4,128,128]{2,0,1:T(4,128)S(1)}, /*index=5*/s32[]{:T(128)}) while((s32[]{:T(128)}, f32[4,128,128]{2,1,0:T(8,128)S(1)}, f32[4,3,49]{2,1,0:T(4,128)S(1)}, ...), condition=%wide.region_16.17_spmd.clone.clone, body=%wide.region_15.16_spmd.clone.clone.sunk | while | flops 557646336 | bytes 6428261 | solution.py:110
  262.5 0.8 select_bitcast_fusion
  (191 shorter events, 59.2 us)
Async XLA Ops:
  7.2 1.8 copy-start
  7.8 0.7 copy-start.8
  7.9 0.7 copy-start.9
  9.8 35.1 %all-to-all-start.1 = ((f32[4,2,1]{1,2,0:T(1,128)}), f32[4,2,1]{1,2,0:T(1,128)S(1)}, u32[]{:S(2)}, u32[]{:S(2)}) async-start(f32[4,2,1]{1,2,0:T(1,128)} %copy.57), calls=%async_computation.1 | async-start | bytes 4096 | tf_op jit(solution)/shard_map/all_to_all | solution.py:79
  22.7 2.7 %copy-start.5 = (f32[1,4,3,49]{3,1,2,0:T(4,128)S(1)}, f32[1,4,3,49]{3,1,2,0:T(4,128)}, u32[]{:S(2)}) copy-start(f32[1,4,3,49]{3,1,2,0:T(4,128)} %param.15) | copy-start | bytes 7060
  26.8 1.0 copy-start.4
  43.5 0.7 copy-start.7
  45.0 10.7 %all-to-all-start = ((f32[4,2,2]{2,1,0:T(2,128)}), f32[4,2,2]{2,1,0:T(2,128)S(1)}, u32[]{:S(2)}, u32[]{:S(2)}) async-start(f32[4,2,2]{2,1,0:T(2,128)} %fusion.28), calls=%async_computation | async-start | bytes 8192 | tf_op jit(solution)/shard_map/all_to_all | solution.py:80
  55.6 16.2 %all-to-all-start.2 = ((f32[8,128,128]{2,1,0:T(8,128)}), f32[8,128,128]{2,1,0:T(8,128)S(1)}, u32[]{:S(2)}, u32[]{:S(2)}) async-start(f32[8,128,128]{2,1,0:T(8,128)} %copy.59), calls=%async_computation.2 | async-start | bytes 1048576 | tf_op jit(solution)/shard_map/all_to_all | solution.py:78
  59.1 145.8 %all-reduce.3.cloned.1.call-start = ((), (), s32[]{:S(2)}) async-start(), calls=%async_computation.4 | async-start | bytes 1048576 | tf_op jit(solution)/shard_map/psum | solution.py:101
  149.2 0.7 copy-start.1
  149.3 0.8 copy-start.2
  226.8 0.7 copy-start.3
  226.8 5.3 %copy-start.6 = (f32[1,4,3,49]{3,1,2,0:T(4,128)S(1)}, f32[1,4,3,49]{3,1,2,0:T(4,128)}, u32[]{:S(2)}) copy-start(f32[1,4,3,49]{3,1,2,0:T(4,128)} %param.16) | copy-start | bytes 7060
  227.5 18.3 %all-to-all-start.3 = ((f32[8,128,128]{2,1,0:T(8,128)}), f32[8,128,128]{2,1,0:T(8,128)S(1)}, u32[]{:S(2)}, u32[]{:S(2)}) async-start(f32[8,128,128]{2,1,0:T(8,128)} %get-tuple-element.193), calls=%async_computation.3 | async-start | bytes 1048576 | tf_op jit(solution)/shard_map/all_to_all | solution.py:106
Sparse Core Ops, SparseCore 0:
  150.2 54.6 all-reduce.2
where the time goes:
time: 271 us; the launch traced here: 270 us
  waiting for transfers between devices  84.3 us (31%)
  local copies, waits for them, and re-layouts  68.5 us (25%)
  loops' own time  33 us (12%)
  matrix products  30.9 us (11%)
  between operations  19.6 us (7%)
  starting transfers between devices  19.5 us (7%)
  other arithmetic  14.3 us (5%)
    psum x1, waiting for transfers between devices, body(): weighted, coverage = lax.psum((weighted, coverage), 'visit')  54.8 us
    another operation x1, loops' own time, body(): lax.fori_loop(0, buffer_slots, place_block, (empty, empty))  32.4 us
    gather x24, local copies, waits for them, and re-layouts  20.8 us
    dynamic_update_slice x8, local copies, waits for them, and re-layouts, place_block(): lax.dynamic_update_slice(coverage, region + block_weight, (corner_top, co...  14.4 us
    dynamic_update_slice x8, local copies, waits for them, and re-layouts, place_block(): lax.dynamic_update_slice(weighted, region + block_weight * arrived[positi...  14.4 us
    all_to_all x1, waiting for transfers between devices, body(): lax.all_to_all(cut_back, 'sky', split_axis=0, concat_axis=0, tiled=True)  13.8 us
    all_to_all x1, waiting for transfers between devices, body(): lax.all_to_all(packed, 'sky', split_axis=0, concat_axis=0, tiled=True)  11.1 us
    all_to_all x1, starting transfers between devices, body(): lax.all_to_all(sent_weight, 'sky', split_axis=0, concat_axis=0, tiled=True)  6.35 us
  transfers between devices with their start and end apart: 5, of which 4 were waited for; matrix products, arithmetic and copies ran while one was open for 9% of the time, Pallas kernels for 0%

commit v1 on v0

--- a/solution.py
+++ b/solution.py
@@ -9,6 +9,28 @@
 WIDTHS = (1.0, 1.0, 1.0, 2.5, 2.5, 2.5, 5.0)
 POWERS = (0, 1, 2, 0, 1, 2, 0)
 PRECISE = lax.Precision.HIGHEST
+
+
+def split_up(array, dim, size):
+    before, after = (array.shape[:dim], array.shape[dim + 1 :])
+    return jnp.moveaxis(array.reshape(*before, size, -1, *after), dim, 0)
+
+
+def joined_along(blocks, dim):
+    lengths = list(blocks.shape[1:])
+    lengths[dim] *= blocks.shape[0]
+    return jnp.moveaxis(blocks, 0, dim).reshape(lengths)
+
+
+def sent_to_each(value, axis, split_dim, concat_dim):
+    devices, index = (lax.axis_size(axis), lax.axis_index(axis))
+    blocks = split_up(value, split_dim, devices)
+    done = [blocks[index]]
+    for step in range(1, devices):
+        sent = blocks[(index + step) % devices]
+        done.append(lax.ppermute(sent, axis, [(i, (i + step) % devices) for i in range(devices)]))
+    blocks = jnp.stack(done)[(index - jnp.arange(devices)) % devices]
+    return joined_along(blocks, concat_dim)
 
 
 def profile_filters(side):
@@ -75,7 +97,7 @@
     sent_weight = jnp.dot(routing, weight[0], precision=PRECISE)
     sent_corner = jnp.dot(routing, offsets[0].astype(jnp.float32), precision=PRECISE)
     arrived, arrived_weight, arrived_corner = (
-        lax.all_to_all(packed, "sky", split_axis=0, concat_axis=0, tiled=True),
+        sent_to_each(packed, "sky", 0, 0),
         lax.all_to_all(sent_weight, "sky", split_axis=0, concat_axis=0, tiled=True),
         lax.all_to_all(sent_corner, "sky", split_axis=0, concat_axis=0, tiled=True),
     )

time: 271 us -> 262 us (0.967)
  waiting for transfers between devices: 84.3 us -> 77.8 us
    all_to_all x1 -> x0, waiting for transfers between devices: 11.1 us -> none  [body(): lax.all_to_all(packed, 'sky', split_axis=0, concat_axis=0, tiled=True)]
    ppermute x0 -> x3, starting transfers between devices: none -> 7.04 us  [sent_to_each(): lax.ppermute(sent, axis, [(i, (i + step) % devices) for i in range(device...]
    all_to_all x1, waiting for transfers between devices: 0.01 us -> 5.04 us  [body(): lax.all_to_all(sent_weight, 'sky', split_axis=0, concat_axis=0, tiled=True)]
    all_to_all x1 -> x0, starting transfers between devices: 3.47 us -> none  [body(): lax.all_to_all(packed, 'sky', split_axis=0, concat_axis=0, tiled=True)]
    all_to_all x1, starting transfers between devices: 6.35 us -> 3.35 us  [body(): lax.all_to_all(sent_weight, 'sky', split_axis=0, concat_axis=0, tiled=True)]
    gather x24 -> x25, local copies, waits for them, and re-layouts: 20.8 us -> 21.4 us
  transfers between devices with their start and end apart: 5 -> 7, of which waited for: 4 -> 4; matrix products, arithmetic and copies ran while one was open for 9% -> 1% of each run, Pallas kernels for 0% -> 0%
where the time goes in v1:
time: 262 us; the launch traced here: 261 us
  waiting for transfers between devices  77.8 us (30%)
  local copies, waits for them, and re-layouts  67.9 us (26%)
  loops' own time  32 us (12%)
  matrix products  30.9 us (12%)
  between operations  19.7 us (8%)
  starting transfers between devices  18.2 us (7%)
  other arithmetic  14.8 us (6%)
    psum x1, waiting for transfers between devices, body(): weighted, coverage = lax.psum((weighted, coverage), 'visit')  54.8 us
    another operation x1, loops' own time, body(): lax.fori_loop(0, buffer_slots, place_block, (empty, empty))  31.4 us
    gather x24, local copies, waits for them, and re-layouts  20.8 us
    dynamic_update_slice x8, local copies, waits for them, and re-layouts, place_block(): lax.dynamic_update_slice(coverage, region + block_weight, (corner_top, co...  14.4 us
    dynamic_update_slice x8, local copies, waits for them, and re-layouts, place_block(): lax.dynamic_update_slice(weighted, region + block_weight * arrived[positi...  14.4 us
    all_to_all x1, waiting for transfers between devices, body(): lax.all_to_all(cut_back, 'sky', split_axis=0, concat_axis=0, tiled=True)  13.8 us
    ppermute x3, starting transfers between devices, sent_to_each(): lax.ppermute(sent, axis, [(i, (i + step) % devices) for i in range(device...  7.04 us
    add x8, other arithmetic, place_block(): region + block_weight * arrived[position]  6.03 us
  transfers between devices with their start and end apart: 7, of which 4 were waited for; matrix products, arithmetic and copies ran while one was open for 1% of the time, Pallas kernels for 0%

profile of v1, /device:TPU:0, one launch (start us, length us, event | category | flops | bytes accessed | tf_op | source)
XLA Modules:
  0.0 261.4 jit_solution(12023912956948725001)
XLA Ops:
  17.9 0.9 copy-done.4
  18.8 15.7 %while.42 = (s32[]{:T(128)}, f32[4,128,128]{2,1,0:T(8,128)S(1)}, f32[4,3,49]{2,1,0:T(4,128)S(1)}, f32[7,128,128]{2,0,1:T(8,128)S(1)}, f32[4,128,128]{2,1,0:T(8,128)S(1)}, /*index=5*/s32[]{:T(128)}) while((s32[]{:T(128)}, f32[4,128,128]{2,1,0:T(8,128)S(1)}, f32[4,3,49]{2,1,0:T(4,128)S(1)}, ...), condition=%wide.region_10.11_spmd.clone.clone, body=%wide.region_9.10_spmd.clone.clone.sunk | while | flops 557646336 | bytes 6362725 | solution.py:84
  37.5 3.1 %collective-permute-start = (f32[2,128,128]{2,1,0:T(8,128)S(1)}, f32[2,128,128]{2,1,0:T(8,128)S(1)}, u32[]{:S(2)}, u32[]{:S(2)}) collective-permute-start(f32[2,128,128]{2,1,0:T(8,128)S(1)} %bitcast.217), channel_id=1, source_target_pairs={{0,1},{1,2},{2,3},{3,0},{4,5},{5,6},{6,7},{7,4},{8,9},{9,10},{10,1... | collective-permute-start | bytes 393224 | tf_op jit(solution)/shard_map/ppermute | solution.py:31
  40.6 2.6 collective-permute-start.1
  43.1 1.4 collective-permute-start.2
  45.4 3.4 %all-to-all-start.1 = ((f32[4,2,1]{1,2,0:T(1,128)}), f32[4,2,1]{1,2,0:T(1,128)S(1)}, u32[]{:S(2)}, u32[]{:S(2)}) async-start(f32[4,2,1]{1,2,0:T(1,128)} %copy.56), calls=%async_computation.1 | async-start | bytes 4096 | tf_op jit(solution)/shard_map/all_to_all | solution.py:101
  49.5 5.0 %all-to-all-done.1 = f32[4,2,1]{1,2,0:T(1,128)S(1)} async-done(((f32[4,2,1]{1,2,0:T(1,128)}), f32[4,2,1]{1,2,0:T(1,128)S(1)}, u32[]{:S(2)}, u32[]{:S(2)}) %all-to-all-start.1) | async-done | bytes 64 | tf_op jit(solution)/shard_map/all_to_all | solution.py:101
  54.6 3.2 %all-to-all-start = ((f32[4,2,2]{2,1,0:T(2,128)}), f32[4,2,2]{2,1,0:T(2,128)S(1)}, u32[]{:S(2)}, u32[]{:S(2)}) async-start(f32[4,2,2]{2,1,0:T(2,128)} %fusion.28), calls=%async_computation | async-start | bytes 8192 | tf_op jit(solution)/shard_map/all_to_all | solution.py:102
  59.1 4.2 %all-to-all-done = f32[4,2,2]{2,1,0:T(2,128)S(1)} async-done(((f32[4,2,2]{2,1,0:T(2,128)}), f32[4,2,2]{2,1,0:T(2,128)S(1)}, u32[]{:S(2)}, u32[]{:S(2)}) %all-to-all-start) | async-done | bytes 96 | tf_op jit(solution)/shard_map/all_to_all | solution.py:102
  64.8 75.6 %while.40 = (s32[]{:T(128)}, f32[256,256]{1,0:T(8,128)S(1)}, f32[256,256]{1,0:T(8,128)S(1)}, s32[8,2]{0,1:T(2,128)S(1)}, f32[8]{0:T(128)S(1)}, /*index=5*/f32[8,...) while((s32[]{:T(128)}, f32[256,256]{1,0:T(8,128)S(1)}, f32[256,256]{1,0:T(8,128)S(1)}, ...), condition=%wide.region_12.13_spmd, body=%wide.region_11.12_spmd.sunk | while | flops 49160 | bytes 591569 | solution.py:122
  69.9 0.8 bitcast_add_fusion.2
  70.7 2.0 dynamic_update_slice.32
  72.7 2.0 dynamic_update_slice.31
  79.7 0.8 bitcast_add_fusion.2
  80.5 1.9 dynamic_update_slice.32
  82.4 1.9 dynamic_update_slice.31
  89.5 0.8 bitcast_add_fusion.2
  90.2 2.0 dynamic_update_slice.32
  92.2 2.0 dynamic_update_slice.31
  99.2 0.8 bitcast_add_fusion.2
  100.0 1.7 dynamic_update_slice.32
  101.7 1.7 dynamic_update_slice.31
  108.4 0.8 bitcast_add_fusion.2
  109.2 1.9 dynamic_update_slice.32
  111.1 1.9 dynamic_update_slice.31
  118.0 0.8 bitcast_add_fusion.2
  118.8 1.7 dynamic_update_slice.32
  120.5 1.7 dynamic_update_slice.31
  127.2 0.8 bitcast_add_fusion.2
  128.0 1.7 dynamic_update_slice.32
  129.6 1.7 dynamic_update_slice.31
  137.1 1.7 dynamic_update_slice.32
  138.8 1.7 dynamic_update_slice.31
  141.3 54.8 %all-reduce.3.cloned.1.call-done = (f32[256,256]{1,0:T(8,128)}, f32[256,256]{1,0:T(8,128)}) async-done(((f32[256,256]{1,0:T(8,128)}, f32[256,256]{1,0:T(8,128)}), (f32[256,256]{1,0:T(8,128)}, f32[256,256]{1,0:T(8,128)})) %all-reduce.3.cloned.1.call-update) | async-done | bytes 524304 | tf_op jit(solution)/shard_map/psum | solution.py:123
  196.1 1.1 add_divide_fusion
  197.2 20.8 %while.41 = (s32[]{:T(128)}, f32[256,256]{1,0:T(8,128)S(1)}, s32[8,2]{0,1:T(2,128)S(1)}, f32[8,128,128]{2,1,0:T(8,128)}, s32[]{:T(128)}) while((s32[]{:T(128)}, f32[256,256]{1,0:T(8,128)S(1)}, s32[8,2]{0,1:T(2,128)S(1)}, f32[8,128,128]{2,1,0:T(8,128)}, s32[]{:T(128)}) %tuple.119), condition=%wide.while_cond, body=%wide.while_body.sunk | while | flops 2 | bytes 132705 | solution.py:126
  197.8 2.0 bitcast_dynamic-update-slice_fusion.2
  200.4 2.0 bitcast_dynamic-update-slice_fusion.2
  203.0 2.0 bitcast_dynamic-update-slice_fusion.2
  205.6 2.0 bitcast_dynamic-update-slice_fusion.2
  208.2 2.0 bitcast_dynamic-update-slice_fusion.2
  210.8 2.0 bitcast_dynamic-update-slice_fusion.2
  213.4 2.0 bitcast_dynamic-update-slice_fusion.2
  216.0 2.0 bitcast_dynamic-update-slice_fusion.2
  218.7 4.6 %all-to-all-start.2 = ((f32[8,128,128]{2,1,0:T(8,128)}), f32[8,128,128]{2,1,0:T(8,128)S(1)}, u32[]{:S(2)}, u32[]{:S(2)}) async-start(f32[8,128,128]{2,1,0:T(8,128)} %get-tuple-element.193), calls=%async_computation.2 | async-start | bytes 1048576 | tf_op jit(solution)/shard_map/all_to_all | solution.py:128
  223.2 13.8 %all-to-all-done.2 = f32[8,128,128]{2,1,0:T(8,128)S(1)} async-done(((f32[8,128,128]{2,1,0:T(8,128)}), f32[8,128,128]{2,1,0:T(8,128)S(1)}, u32[]{:S(2)}, u32[]{:S(2)}) %all-to-all-start.2) | async-done | bytes 524320 | tf_op jit(solution)/shard_map/all_to_all | solution.py:128
  237.7 16.0 %while.43 = (s32[]{:T(128)}, f32[4,128,128]{2,1,0:T(8,128)S(1)}, f32[4,3,49]{2,1,0:T(4,128)S(1)}, f32[7,128,128]{2,0,1:T(8,128)S(1)}, f32[4,128,128]{2,0,1:T(4,128)S(1)}, /*index=5*/s32[]{:T(128)}) while((s32[]{:T(128)}, f32[4,128,128]{2,1,0:T(8,128)S(1)}, f32[4,3,49]{2,1,0:T(4,128)S(1)}, ...), condition=%wide.region_16.17_spmd.clone.clone, body=%wide.region_15.16_spmd.clone.clone.sunk | while | flops 557646336 | bytes 6428261 | solution.py:132
  253.7 0.8 select_bitcast_fusion
  (200 shorter events, 60.8 us)
Async XLA Ops:
  7.2 37.3 %copy-start = (f32[1,4]{1,0:T(1,128)S(1)}, f32[1,4]{1,0:T(1,128)}, u32[]{:S(2)}) copy-start(f32[1,4]{1,0:T(1,128)} %param.17) | copy-start | bytes 52
  12.4 4.1 %copy-start.5 = (f32[1,4,3,49]{3,1,2,0:T(4,128)S(1)}, f32[1,4,3,49]{3,1,2,0:T(4,128)}, u32[]{:S(2)}) copy-start(f32[1,4,3,49]{3,1,2,0:T(4,128)} %param.15) | copy-start | bytes 7060
  17.9 1.0 copy-start.4
  35.2 0.7 copy-start.8
  35.3 0.7 copy-start.9
  37.5 26.2 %collective-permute-start = (f32[2,128,128]{2,1,0:T(8,128)S(1)}, f32[2,128,128]{2,1,0:T(8,128)S(1)}, u32[]{:S(2)}, u32[]{:S(2)}) collective-permute-start(f32[2,128,128]{2,1,0:T(8,128)S(1)} %bitcast.217), channel_id=1, source_target_pairs={{0,1},{1,2},{2,3},{3,0},{4,5},{5,6},{6,7},{7,4},{8,9},{9,10},{10,1... | collective-permute-start | bytes 393224 | tf_op jit(solution)/shard_map/ppermute | solution.py:31
  40.6 23.1 %collective-permute-start.1 = (f32[2,128,128]{2,1,0:T(8,128)S(1)}, f32[2,128,128]{2,1,0:T(8,128)S(1)}, u32[]{:S(2)}, u32[]{:S(2)}) collective-permute-start(f32[2,128,128]{2,1,0:T(8,128)S(1)} %bitcast.215), channel_id=1, source_target_pairs={{0,2},{1,3},{2,0},{3,1},{4,6},{5,7},{6,4},{7,5},{8,10},{9,11},{10,... | collective-permute-start | bytes 393224 | tf_op jit(solution)/shard_map/ppermute | solution.py:31
  43.1 20.5 %collective-permute-start.2 = (f32[2,128,128]{2,1,0:T(8,128)S(1)}, f32[2,128,128]{2,1,0:T(8,128)S(1)}, u32[]{:S(2)}, u32[]{:S(2)}) collective-permute-start(f32[2,128,128]{2,1,0:T(8,128)S(1)} %bitcast.214), channel_id=1, source_target_pairs={{0,3},{1,0},{2,1},{3,2},{4,7},{5,4},{6,5},{7,6},{8,11},{9,8},{10,9... | collective-permute-start | bytes 393224 | tf_op jit(solution)/shard_map/ppermute | solution.py:31
  45.4 3.4 %copy-start.7 = (s32[1,4,2]{1,2,0:T(2,128)S(1)}, s32[1,4,2]{1,2,0:T(2,128)}, u32[]{:S(2)}) copy-start(s32[1,4,2]{1,2,0:T(2,128)} %param.19) | copy-start | bytes 100
  45.4 9.2 %all-to-all-start.1 = ((f32[4,2,1]{1,2,0:T(1,128)}), f32[4,2,1]{1,2,0:T(1,128)S(1)}, u32[]{:S(2)}, u32[]{:S(2)}) async-start(f32[4,2,1]{1,2,0:T(1,128)} %copy.56), calls=%async_computation.1 | async-start | bytes 4096 | tf_op jit(solution)/shard_map/all_to_all | solution.py:101
  54.6 8.8 %all-to-all-start = ((f32[4,2,2]{2,1,0:T(2,128)}), f32[4,2,2]{2,1,0:T(2,128)S(1)}, u32[]{:S(2)}, u32[]{:S(2)}) async-start(f32[4,2,2]{2,1,0:T(2,128)} %fusion.28), calls=%async_computation | async-start | bytes 8192 | tf_op jit(solution)/shard_map/all_to_all | solution.py:102
  57.8 138.3 %all-reduce.3.cloned.1.call-start = ((), (), s32[]{:S(2)}) async-start(), calls=%async_computation.3 | async-start | bytes 1048576 | tf_op jit(solution)/shard_map/psum | solution.py:123
  140.5 0.7 copy-start.1
  140.5 0.8 copy-start.2
  218.0 0.7 copy-start.3
  218.0 5.3 %copy-start.6 = (f32[1,4,3,49]{3,1,2,0:T(4,128)S(1)}, f32[1,4,3,49]{3,1,2,0:T(4,128)}, u32[]{:S(2)}) copy-start(f32[1,4,3,49]{3,1,2,0:T(4,128)} %param.16) | copy-start | bytes 7060
  218.7 18.3 %all-to-all-start.2 = ((f32[8,128,128]{2,1,0:T(8,128)}), f32[8,128,128]{2,1,0:T(8,128)S(1)}, u32[]{:S(2)}, u32[]{:S(2)}) async-start(f32[8,128,128]{2,1,0:T(8,128)} %get-tuple-element.193), calls=%async_computation.2 | async-start | bytes 1048576 | tf_op jit(solution)/shard_map/all_to_all | solution.py:128
Sparse Core Ops, SparseCore 0:
  141.4 54.6 all-reduce.2
